TPU v7x, 128 devices: a whole 4x4x4 slice. The times are simulated.
128 devices in a mesh: agent: 8 (over z, core), chan: 8 (over y, x_hi), batch: 2 (over x_lo).
Axes of the slice: x: 4 (x_hi: 2, x_lo: 2; x = x_hi * 2 + x_lo), y: 4, z: 4, core: 2. Of those that a mesh axis runs over, the one named last changes fastest.
Arguments:
- features: bfloat16 [256, 16, 16384], P(None, None, ('agent', 'chan', 'batch')), may hold values from -6 to 6
- norm_gain: float32 [256], replicated, may hold values from 0.1 to 1.9
- tok_in: bfloat16 [16384, 2048], P('agent'), may hold values from -0.046875 to 0.046875
- tok_out: bfloat16 [2048, 16384], P(None, 'agent'), may hold values from -0.125 to 0.125
- mix_gain: float32 [256], replicated, may hold values from 0.1 to 1.9
- chan_in: bfloat16 [256, 1024], replicated, may hold values from -0.375 to 0.375
- chan_out: bfloat16 [1024, 256], replicated, may hold values from -0.1875 to 0.1875
- head: bfloat16 [256, 8], replicated, may hold values from -8 to 8
- actions: int32 [16, 16384], P(None, ('agent', 'chan', 'batch')), may hold values from 0 to 7
- order: int32 [16384], P(('agent', 'chan', 'batch')), may hold values from 0 to 16383, as said below
Outputs:
- input_grad: float32 [256, 16, 16384], P(None, None, ('agent', 'chan', 'batch'))
- head_grad: float32 [256, 8], replicated
Inputs may be any that keep to these rules, and one draw needn't show every extreme that they name: order maps each aligned block of 128 agents one to one onto the same block.
All inputs are finite; a program needn't handle non-finite values.
Results may differ from a plain program's by a relative error of at most 0.025.
Values may be sent and summed in bfloat16 or wider, within the bound.
A program may use at most 128 MiB of HBM per device.

v0:
```python
import jax
import jax.numpy as jnp
from jax import lax
from jax.sharding import PartitionSpec as P

A = 16384
GELU_K = 0.7978845608028654
GELU_C = 0.044715
EPS = 1e-05


def gelu_value(v):
    return 0.5 * v * (1.0 + jnp.tanh(GELU_K * (v + GELU_C * v * v * v)))


def gelu_slope(v):
    inner = jnp.tanh(GELU_K * (v + GELU_C * v * v * v))
    return 0.5 * (1.0 + inner) + 0.5 * v * (1.0 - inner * inner) * GELU_K * (
        1.0 + 3.0 * GELU_C * v * v
    )


def shaped_gain(gain, field):
    return gain.reshape((gain.shape[0],) + (1,) * (field.ndim - 1))


def norm_forward(field, gain):
    center = jnp.mean(field, axis=0, keepdims=True)
    spread = jnp.mean(jnp.square(field - center), axis=0, keepdims=True)
    scale = lax.rsqrt(spread + EPS)
    unit = (field - center) * scale
    return (unit * shaped_gain(gain, field), unit, scale)


def norm_backward(upstream, gain, unit, scale):
    weighted = upstream * shaped_gain(gain, upstream)
    return scale * (
        weighted
        - jnp.mean(weighted, axis=0, keepdims=True)
        - unit * jnp.mean(weighted * unit, axis=0, keepdims=True)
    )


def to_tokens(field):
    return lax.all_to_all(field, ("chan", "batch"), split_axis=0, concat_axis=2, tiled=True)


def to_channels(field):
    return lax.all_to_all(field, ("chan", "batch"), split_axis=2, concat_axis=0, tiled=True)


def project(weight, hidden_dim, rows):
    agent_dim = 1 - hidden_dim
    partial_sum = lax.dot_general(
        weight, rows, (((agent_dim,), (1,)), ((), ())), preferred_element_type=jnp.float32
    )
    return lax.psum(partial_sum, "agent")


def expand(spread, weight, hidden_dim):
    return lax.dot_general(
        spread, weight, (((0,), (hidden_dim,)), ((), ())), preferred_element_type=jnp.float32
    )


def shards(features, norm_gain, tok_in, tok_out, mix_gain, chan_in, chan_out, head, actions, order):
    wide = features.astype(jnp.float32)
    chans, samples, local = wide.shape
    normed_in, unit_in, scale_in = norm_forward(wide, norm_gain)
    spread_in = to_tokens(normed_in.astype(jnp.bfloat16))
    token_chans, _, agents = spread_in.shape
    token_rows = spread_in.reshape(token_chans * samples, agents)
    hidden_pre = project(tok_in, 1, token_rows)
    hidden_act = gelu_value(hidden_pre).astype(jnp.bfloat16)
    mixed = (
        expand(hidden_act, tok_out, 0).astype(jnp.bfloat16).reshape(token_chans, samples, agents)
    )
    mixed_back = to_channels(mixed)
    first = wide + mixed_back.astype(jnp.float32)
    normed_mid, unit_mid, scale_mid = norm_forward(first, mix_gain)
    flat_mid = normed_mid.astype(jnp.bfloat16).reshape(chans, samples * local)
    inner_pre = lax.dot_general(
        chan_in, flat_mid, (((0,), (0,)), ((), ())), preferred_element_type=jnp.float32
    )
    inner = gelu_value(inner_pre).astype(jnp.bfloat16)
    outer = lax.dot_general(
        chan_out, inner, (((0,), (0,)), ((), ())), preferred_element_type=jnp.float32
    )
    second = (first.reshape(chans, samples * local) + outer).astype(jnp.bfloat16)
    logits = lax.dot_general(
        head, second, (((0,), (0,)), ((), ())), preferred_element_type=jnp.float32
    )
    target = jnp.take_along_axis(actions, (order % local)[None, :], axis=1).reshape(
        1, samples * local
    )
    phases = lax.broadcasted_iota(jnp.int32, logits.shape, 0)
    picked = (phases == target).astype(jnp.float32)
    top = jnp.max(logits, axis=0, keepdims=True)
    exps = jnp.exp(logits - top)
    probs = exps / jnp.sum(exps, axis=0, keepdims=True)
    slope = (probs - picked).astype(jnp.bfloat16)
    head_part = lax.dot_general(
        second, slope, (((1,), (1,)), ((), ())), preferred_element_type=jnp.float32
    )
    head_total = lax.psum(head_part, ("agent", "chan", "batch"))
    head_grad = head_total * (1.0 / (samples * A))
    back_second = lax.dot_general(
        head, slope, (((1,), (0,)), ((), ())), preferred_element_type=jnp.float32
    )
    back_low = back_second.astype(jnp.bfloat16)
    back_inner = lax.dot_general(
        chan_out, back_low, (((1,), (0,)), ((), ())), preferred_element_type=jnp.float32
    )
    back_inner_pre = (back_inner * gelu_slope(inner_pre)).astype(jnp.bfloat16)
    back_mid = lax.dot_general(
        chan_in, back_inner_pre, (((1,), (0,)), ((), ())), preferred_element_type=jnp.float32
    )
    back_first = back_second.reshape(chans, samples, local) + norm_backward(
        back_mid.reshape(chans, samples, local), mix_gain, unit_mid, scale_mid
    )
    back_tokens = to_tokens(back_first.astype(jnp.bfloat16))
    back_rows = back_tokens.reshape(token_chans * samples, agents)
    back_hidden = project(tok_out, 0, back_rows)
    back_hidden_pre = (back_hidden * gelu_slope(hidden_pre)).astype(jnp.bfloat16)
    back_spread = (
        expand(back_hidden_pre, tok_in, 1)
        .astype(jnp.bfloat16)
        .reshape(token_chans, samples, agents)
    )
    back_norm = to_channels(back_spread)
    input_grad = back_first + norm_backward(
        back_norm.astype(jnp.float32), norm_gain, unit_in, scale_in
    )
    return (input_grad, head_grad)


def solution(mesh):
    in_specs = (
        P(None, None, ("agent", "chan", "batch")),
        P(),
        P("agent", None),
        P(None, "agent"),
        P(),
        P(),
        P(),
        P(),
        P(None, ("agent", "chan", "batch")),
        P(("agent", "chan", "batch")),
    )
    out_specs = (P(None, None, ("agent", "chan", "batch")), P())
    return jax.shard_map(shards, mesh=mesh, in_specs=in_specs, out_specs=out_specs, check_vma=False)
```

profile of v0, /device:TPU:1, one launch (start us, length us, event | category | flops | bytes accessed | tf_op | source)
XLA Modules:
  0.0 469.4 jit_solution(13224073951282337597)
XLA Ops:
  10.8 23.5 %all_to_all.48 = bf16[256,16,128]{2,1,0:T(8,128)(2,1)S(1)} all-to-all(bf16[256,16,128]{2,1,0:T(8,128)(2,1)S(1)} %fusion.16), channel_id=1, replica_groups=mesh['agent'=8,'chan'=8,'batch'=2] {'chan','batch'}, dimensions={0} | all-to-all | bytes 2097152 | tf_op jit(solution)/shard_map/all_to_all | solution.py:45
  35.0 7.0 %convolution_bitcast_fusion.1 = f32[2048,256]{0,1:T(8,128)} fusion(bf16[2048,2048]{1,0:T(8,128)(2,1)} %param.12, bf16[32,8,16,128]{3,2,1,0:T(8,128)(2,1)S(1)} %bitcast.134), kind=kOutput, calls=%fused_computation.23 | convolution fusion | flops 2147483648 | bytes 11534336 | tf_op jit(solution)/shard_map/dot_general | solution.py:54
  42.1 64.0 %all-reduce.3.cloned.1.call-done = f32[2048,256]{0,1:T(8,128)} async-done(((f32[2048,256]{0,1:T(8,128)}), f32[2048,256]{0,1:T(8,128)}) %all-reduce.3.cloned.1.call-update) | async-done | bytes 2097168 | tf_op jit(solution)/shard_map/psum | solution.py:57
  106.1 6.6 %convolution_convert_fusion.1 = bf16[256,2048]{1,0:T(8,128)(2,1)S(1)} fusion(bf16[2048,2048]{1,0:T(8,128)(2,1)} %param.13, f32[2048,256]{0,1:T(8,128)} %all-reduce.3.cloned.1.call-done), kind=kOutput, calls=%fused_computation.27 | convolution fusion | flops 2152726528 | bytes 11534336 | tf_op jit(solution)/shard_map/dot_general | solution.py:61
  112.6 8.5 %copy.57 = bf16[16,16,2048]{1,0,2:T(8,128)(2,1)} copy(bf16[16,16,2048]{2,1,0:T(8,128)(2,1)S(1)} %bitcast.133) | data formatting | bytes 2097152 | tf_op jit(solution)/shard_map/reshape | solution.py:76
  121.1 11.2 %reshape.152 = bf16[16,2,16384]{2,1,0:T(2,128)(2,1)} reshape(bf16[2048,16,16]{2,1,0:T(8,128)(2,1)} %bitcast.124) | data formatting | bytes 2097152
  132.4 6.7 %all-to-all-start.1 = ((bf16[16,2,16384]{2,1,0:T(2,128)(2,1)}), bf16[16,2,16384]{2,1,0:T(2,128)(2,1)S(1)}, u32[]{:S(2)}, u32[]{:S(2)}) async-start(bf16[16,2,16384]{2,1,0:T(2,128)(2,1)} %reshape.152), calls=%async_computation.1 | async-start | bytes 2097152 | tf_op jit(solution)/shard_map/all_to_all | solution.py:49
  140.5 13.1 %all-to-all-done.1 = bf16[16,2,16384]{2,1,0:T(2,128)(2,1)S(1)} async-done(((bf16[16,2,16384]{2,1,0:T(2,128)(2,1)}), bf16[16,2,16384]{2,1,0:T(2,128)(2,1)S(1)}, u32[]{:S(2)}, u32[]{:S(2)}) %all-to-all-start.1) | async-done | bytes 1048608 | tf_op jit(solution)/shard_map/all_to_all | solution.py:49
  153.6 7.5 %reshape.153 = bf16[2048,16,16]{2,1,0:T(8,128)(2,1)} reshape(bf16[16,2,16384]{2,1,0:T(2,128)(2,1)S(1)} %all-to-all-done.1) | data formatting | bytes 2097152
  161.1 10.9 %convert_bitcast_fusion = f32[16,16,16,128]{2,1,3,0:T(8,128)} fusion(bf16[16,16,16,128]{1,0,3,2:T(8,128)(2,1)} %bitcast.123), kind=kLoop, calls=%fused_computation.1 | loop fusion | flops 524288 | bytes 3145728 | tf_op jit(solution)/shard_map/convert_element_type | solution.py:79
  172.0 11.4 %copy.58 = f32[16,16,16,128]{3,2,1,0:T(8,128)} copy(f32[16,16,16,128]{2,1,3,0:T(8,128)} %convert_bitcast_fusion) | data formatting | bytes 4194304 | tf_op jit(solution)/shard_map/convert_element_type | solution.py:79
  196.0 9.5 %fusion.29 = (f32[2048]{0:T(1024)S(1)}, f32[2048,256]{1,0:T(8,128)}) fusion(f32[256]{0:T(256)S(1)} %copy-done.13, bf16[256,1024]{1,0:T(8,128)(2,1)S(1)} %copy-done, f32[2048,1024]{1,0:T(8,128)} %copy-done.6, bf16[1024,256]{1,0:T(8,128)(2,1)S(1)} %copy-done.15, f32[2048,256]{1,0:T(8,128)} %fusion.71), kind=kOutput, calls=%fused_computation.48 | convolution fusion | flops 2188376064 | bytes 13640704 | tf_op jit(solution)/shard_map/dot_general | solution.py:115
  216.7 17.1 %all_to_all.49 = bf16[256,16,128]{2,1,0:T(8,128)(2,1)S(1)} all-to-all(bf16[256,16,128]{2,1,0:T(8,128)(2,1)S(1)} %get-tuple-element.2), channel_id=1, replica_groups=mesh['agent'=8,'chan'=8,'batch'=2] {'chan','batch'}, dimensions={0} | all-to-all | bytes 2097152 | tf_op jit(solution)/shard_map/all_to_all | solution.py:45
  234.5 7.0 %convolution_bitcast_fusion = f32[2048,256]{0,1:T(8,128)} fusion(bf16[2048,2048]{1,0:T(8,128)(2,1)} %param.13, bf16[32,8,16,128]{3,2,1,0:T(8,128)(2,1)S(1)} %bitcast.135), kind=kOutput, calls=%fused_computation.22 | convolution fusion | flops 2147483648 | bytes 11534336 | tf_op jit(solution)/shard_map/dot_general | solution.py:54
  241.5 70.8 %all-reduce.5.cloned.1.call-done = f32[2048,256]{0,1:T(8,128)} async-done(((f32[2048,256]{0,1:T(8,128)}), f32[2048,256]{0,1:T(8,128)}) %all-reduce.5.cloned.1.call-update) | async-done | bytes 2097168 | tf_op jit(solution)/shard_map/psum | solution.py:57
  312.3 7.8 %convolution_convert_fusion = bf16[256,2048]{1,0:T(8,128)(2,1)S(1)} fusion(bf16[2048,2048]{1,0:T(8,128)(2,1)} %param.12, f32[2048,256]{0,1:T(8,128)} %all-reduce.5.cloned.1.call-done, f32[2048,256]{0,1:T(8,128)} %all-reduce.3.cloned.1.call-done), kind=kOutput, calls=%fused_computation.26 | convolution fusion | flops 2157969408 | bytes 13631488 | tf_op jit(solution)/shard_map/dot_general | solution.py:61
  320.1 8.5 %copy.65 = bf16[16,16,2048]{1,0,2:T(8,128)(2,1)} copy(bf16[16,16,2048]{2,1,0:T(8,128)(2,1)S(1)} %bitcast.132) | data formatting | bytes 2097152 | tf_op jit(solution)/shard_map/reshape | solution.py:128
  328.6 11.2 %reshape.154 = bf16[16,2,16384]{2,1,0:T(2,128)(2,1)} reshape(bf16[2048,16,16]{2,1,0:T(8,128)(2,1)} %bitcast.125) | data formatting | bytes 2097152
  339.9 6.7 %all-to-all-start.3 = ((bf16[16,2,16384]{2,1,0:T(2,128)(2,1)}), bf16[16,2,16384]{2,1,0:T(2,128)(2,1)S(1)}, u32[]{:S(2)}, u32[]{:S(2)}) async-start(bf16[16,2,16384]{2,1,0:T(2,128)(2,1)} %reshape.154), calls=%async_computation.3 | async-start | bytes 2097152 | tf_op jit(solution)/shard_map/all_to_all | solution.py:49
  346.9 73.3 %psum.23 = f32[256,8]{0,1:T(8,128)S(1)} all-reduce(f32[256,8]{0,1:T(8,128)S(1)} %fusion.69), channel_id=1, replica_groups=mesh['agent'=8,'chan'=8,'batch'=2] {'agent','chan','batch'}, use_global_device_ids=true, to_apply=%region_12.13 | all-reduce | flops 2048 | bytes 16384 | tf_op jit(solution)/shard_map/psum | solution.py:105
  420.8 7.5 %reshape.155 = bf16[2048,16,16]{2,1,0:T(8,128)(2,1)} reshape(bf16[16,2,16384]{2,1,0:T(2,128)(2,1)S(1)} %all-to-all-done.3) | data formatting | bytes 2097152
  428.3 10.9 %convert_bitcast_fusion.1 = f32[16,16,16,128]{2,1,3,0:T(8,128)} fusion(bf16[2048,16,16]{2,1,0:T(8,128)(2,1)} %reshape.155), kind=kLoop, calls=%fused_computation.2 | loop fusion | flops 524288 | bytes 3145728 | tf_op jit(solution)/shard_map/convert_element_type | solution.py:132
  439.2 5.7 %multiply_reduce_fusion = f32[16,128]{0,1:T(8,128)S(1)} fusion(f32[16,16]{1,0:T(8,128)S(1)} %mul.242, bf16[16,16,16,128]{1,0,3,2:T(8,128)(2,1)} %bitcast.122), kind=kLoop, calls=%fused_computation.3 | loop fusion | flops 1570816 | bytes 1057792 | tf_op jit(solution)/shard_map/reduce_sum | solution.py:39
  445.0 11.5 %copy.66 = f32[16,16,16,128]{3,2,1,0:T(8,128)} copy(f32[16,16,16,128]{2,1,3,0:T(8,128)} %convert_bitcast_fusion.1) | data formatting | bytes 4194304 | tf_op jit(solution)/shard_map/convert_element_type | solution.py:132
  (76 shorter events, 36.9 us)
Async XLA Ops:
  7.2 181.3 %copy-start = (bf16[256,1024]{1,0:T(8,128)(2,1)S(1)}, bf16[256,1024]{1,0:T(8,128)(2,1)}, u32[]{:S(2)}) copy-start(bf16[256,1024]{1,0:T(8,128)(2,1)} %param.15) | copy-start | bytes 1572868
  7.2 3.2 copy-start.2
  7.2 3.2 copy-start.12
  7.2 98.9 %all-reduce.3.cloned.1.call-start = ((), (), s32[]{:S(2)}) async-start(), calls=%async_computation.4 | async-start | bytes 4194304 | tf_op jit(solution)/shard_map/psum | solution.py:57
  132.4 7.2 %copy-start.14 = (s32[16,128]{1,0:T(8,128)S(1)}, s32[16,128]{1,0:T(8,128)}, u32[]{:S(2)}) copy-start(s32[16,128]{1,0:T(8,128)} %param.18) | copy-start | bytes 24580
  132.4 7.3 %copy-start.16 = (s32[128]{0:T(128)S(1)}, s32[128]{0:T(128)}, u32[]{:S(2)}) copy-start(s32[128]{0:T(128)} %param.19) | copy-start | bytes 1540
  132.4 21.2 %all-to-all-start.1 = ((bf16[16,2,16384]{2,1,0:T(2,128)(2,1)}), bf16[16,2,16384]{2,1,0:T(2,128)(2,1)S(1)}, u32[]{:S(2)}, u32[]{:S(2)}) async-start(bf16[16,2,16384]{2,1,0:T(2,128)(2,1)} %reshape.152), calls=%async_computation.1 | async-start | bytes 2097152 | tf_op jit(solution)/shard_map/all_to_all | solution.py:49
  139.0 173.2 %all-reduce.5.cloned.1.call-start = ((), (), s32[]{:S(2)}) async-start(), calls=%async_computation.5 | async-start | bytes 4194304 | tf_op jit(solution)/shard_map/psum | solution.py:57
  187.4 0.7 copy-start.13
  188.4 1.6 copy-start.10
  188.5 1.7 copy-start.15
  189.8 3.3 copy-start.6
  190.1 3.0 copy-start.11
  193.2 1.0 copy-start.8
  211.8 2.2 copy-start.4
  211.8 2.8 copy-start.7
  339.9 6.7 %copy-start.9 = (bf16[256,2048]{0,1:T(8,128)(2,1)S(1)}, bf16[256,2048]{0,1:T(8,128)(2,1)}, u32[]{:S(2)}) copy-start(bf16[256,2048]{0,1:T(8,128)(2,1)} %copy-done.8) | copy-start | bytes 3145732
  339.9 80.9 %all-to-all-start.3 = ((bf16[16,2,16384]{2,1,0:T(2,128)(2,1)}), bf16[16,2,16384]{2,1,0:T(2,128)(2,1)S(1)}, u32[]{:S(2)}, u32[]{:S(2)}) async-start(bf16[16,2,16384]{2,1,0:T(2,128)(2,1)} %reshape.154), calls=%async_computation.3 | async-start | bytes 2097152 | tf_op jit(solution)/shard_map/all_to_all | solution.py:49
  444.9 11.5 %copy-start.3 = (bf16[256,16,128]{2,1,0:T(8,128)(2,1)S(1)}, bf16[256,16,128]{2,1,0:T(8,128)(2,1)}, u32[]{:S(2)}) copy-start(bf16[256,16,128]{2,1,0:T(8,128)(2,1)} %param.10) | copy-start | bytes 3145732
  456.5 2.2 copy-start.5
  458.7 3.6 copy-start.1
Sparse Core Ops, SparseCore 0:
  42.2 63.8 all-reduce.2
  241.7 70.5 all-reduce.4
where the time goes:
time: 477 us; the launch traced here: 469 us
  waiting for transfers between devices  148 us (31%)
  blocking collectives  114 us (24%)
  local copies, waits for them, and re-layouts  89.9 us (19%)
  matrix products  44.8 us (9%)
  other arithmetic  44.6 us (9%)
  between operations  14.6 us (3%)
  starting transfers between devices  13.9 us (3%)
    psum x2, waiting for transfers between devices, project(): return lax.psum(partial_sum, 'agent')  135 us
    psum x1, blocking collectives, shards(): head_total = lax.psum(head_part, ('agent', 'chan', 'batch'))  73.3 us
    all_to_all x2, blocking collectives, to_tokens(): lax.all_to_all(field, ('chan', 'batch'), split_axis=0, concat_axis=2, til...  40.6 us
    unnamed x39, local copies, waits for them, and re-layouts  39.6 us
    dot_general x2, matrix products, expand(): lax.dot_general(spread, weight, (((0,), (hidden_dim,)), ((), ())), prefer...  14.4 us
    dot_general x2, matrix products, project(): lax.dot_general(weight, rows, (((agent_dim,), (1,)), ((), ())), preferred...  14.1 us
    all_to_all x2, starting transfers between devices, to_channels(): lax.all_to_all(field, ('chan', 'batch'), split_axis=2, concat_axis=0, til...  13.3 us
    all_to_all x2, waiting for transfers between devices, to_channels(): lax.all_to_all(field, ('chan', 'batch'), split_axis=2, concat_axis=0, til...  13.1 us
  transfers between devices with their start and end apart: 4, of which 3 were waited for; matrix products, arithmetic and copies ran while one was open for 0% of the time, Pallas kernels for 0%

commit v1 on v0

--- a/solution.py
+++ b/solution.py
@@ -102,7 +102,7 @@
     head_part = lax.dot_general(
         second, slope, (((1,), (1,)), ((), ())), preferred_element_type=jnp.float32
     )
-    head_total = lax.psum(head_part, ("agent", "chan", "batch"))
+    head_total = lax.psum(lax.psum(head_part, "agent"), ("chan", "batch"))
     head_grad = head_total * (1.0 / (samples * A))
     back_second = lax.dot_general(
         head, slope, (((1,), (0,)), ((), ())), preferred_element_type=jnp.float32

time: 477 us -> 453 us (0.950)
  blocking collectives: 114 us -> 89.7 us
    psum x1 -> x2, blocking collectives: 73.3 us -> 49.1 us  [shards(): head_total = lax.psum(lax.psum(head_part, 'agent'), ('chan', 'batch'))]
where the time goes in v1:
time: 453 us; the launch traced here: 445 us
  waiting for transfers between devices  148 us (33%)
  local copies, waits for them, and re-layouts  89.7 us (20%)
  blocking collectives  89.7 us (20%)
  matrix products  44.8 us (10%)
  other arithmetic  44.6 us (10%)
  between operations  14.3 us (3%)
  starting transfers between devices  13.6 us (3%)
    psum x2, waiting for transfers between devices, project(): return lax.psum(partial_sum, 'agent')  135 us
    psum x2, blocking collectives, shards(): head_total = lax.psum(lax.psum(head_part, 'agent'), ('chan', 'batch'))  49.1 us
    all_to_all x2, blocking collectives, to_tokens(): lax.all_to_all(field, ('chan', 'batch'), split_axis=0, concat_axis=2, til...  40.6 us
    unnamed x39, local copies, waits for them, and re-layouts  39.7 us
    dot_general x2, matrix products, expand(): lax.dot_general(spread, weight, (((0,), (hidden_dim,)), ((), ())), prefer...  14.4 us
    dot_general x2, matrix products, project(): lax.dot_general(weight, rows, (((agent_dim,), (1,)), ((), ())), preferred...  14.1 us
    all_to_all x2, waiting for transfers between devices, to_channels(): lax.all_to_all(field, ('chan', 'batch'), split_axis=2, concat_axis=0, til...  13.4 us
    all_to_all x2, starting transfers between devices, to_channels(): lax.all_to_all(field, ('chan', 'batch'), split_axis=2, concat_axis=0, til...  13.3 us
  transfers between devices with their start and end apart: 4, of which 3 were waited for; matrix products, arithmetic and copies ran while one was open for 0% of the time, Pallas kernels for 0%

profile of v1, /device:TPU:1, one launch (start us, length us, event | category | flops | bytes accessed | tf_op | source)
XLA Modules:
  0.0 444.8 jit_solution(11546553291443644752)
XLA Ops:
  10.8 23.5 %all_to_all.48 = bf16[256,16,128]{2,1,0:T(8,128)(2,1)S(1)} all-to-all(bf16[256,16,128]{2,1,0:T(8,128)(2,1)S(1)} %fusion.16), channel_id=1, replica_groups=mesh['agent'=8,'chan'=8,'batch'=2] {'chan','batch'}, dimensions={0} | all-to-all | bytes 2097152 | tf_op jit(solution)/shard_map/all_to_all | solution.py:45
  35.0 7.0 %convolution_bitcast_fusion.1 = f32[2048,256]{0,1:T(8,128)} fusion(bf16[2048,2048]{1,0:T(8,128)(2,1)} %param.12, bf16[32,8,16,128]{3,2,1,0:T(8,128)(2,1)S(1)} %bitcast.134), kind=kOutput, calls=%fused_computation.23 | convolution fusion | flops 2147483648 | bytes 11534336 | tf_op jit(solution)/shard_map/dot_general | solution.py:54
  42.1 64.0 %all-reduce.3.cloned.1.call-done = f32[2048,256]{0,1:T(8,128)} async-done(((f32[2048,256]{0,1:T(8,128)}), f32[2048,256]{0,1:T(8,128)}) %all-reduce.3.cloned.1.call-update) | async-done | bytes 2097168 | tf_op jit(solution)/shard_map/psum | solution.py:57
  106.1 6.6 %convolution_convert_fusion.1 = bf16[256,2048]{1,0:T(8,128)(2,1)S(1)} fusion(bf16[2048,2048]{1,0:T(8,128)(2,1)} %param.13, f32[2048,256]{0,1:T(8,128)} %all-reduce.3.cloned.1.call-done), kind=kOutput, calls=%fused_computation.27 | convolution fusion | flops 2152726528 | bytes 11534336 | tf_op jit(solution)/shard_map/dot_general | solution.py:61
  112.6 8.5 %copy.57 = bf16[16,16,2048]{1,0,2:T(8,128)(2,1)} copy(bf16[16,16,2048]{2,1,0:T(8,128)(2,1)S(1)} %bitcast.133) | data formatting | bytes 2097152 | tf_op jit(solution)/shard_map/reshape | solution.py:76
  121.1 11.2 %reshape.152 = bf16[16,2,16384]{2,1,0:T(2,128)(2,1)} reshape(bf16[2048,16,16]{2,1,0:T(8,128)(2,1)} %bitcast.124) | data formatting | bytes 2097152
  132.4 6.7 %all-to-all-start.1 = ((bf16[16,2,16384]{2,1,0:T(2,128)(2,1)}), bf16[16,2,16384]{2,1,0:T(2,128)(2,1)S(1)}, u32[]{:S(2)}, u32[]{:S(2)}) async-start(bf16[16,2,16384]{2,1,0:T(2,128)(2,1)} %reshape.152), calls=%async_computation.1 | async-start | bytes 2097152 | tf_op jit(solution)/shard_map/all_to_all | solution.py:49
  140.2 13.4 %all-to-all-done.1 = bf16[16,2,16384]{2,1,0:T(2,128)(2,1)S(1)} async-done(((bf16[16,2,16384]{2,1,0:T(2,128)(2,1)}), bf16[16,2,16384]{2,1,0:T(2,128)(2,1)S(1)}, u32[]{:S(2)}, u32[]{:S(2)}) %all-to-all-start.1) | async-done | bytes 1048608 | tf_op jit(solution)/shard_map/all_to_all | solution.py:49
  153.6 7.5 %reshape.153 = bf16[2048,16,16]{2,1,0:T(8,128)(2,1)} reshape(bf16[16,2,16384]{2,1,0:T(2,128)(2,1)S(1)} %all-to-all-done.1) | data formatting | bytes 2097152
  161.1 10.9 %convert_bitcast_fusion = f32[16,16,16,128]{2,1,3,0:T(8,128)} fusion(bf16[16,16,16,128]{1,0,3,2:T(8,128)(2,1)} %bitcast.123), kind=kLoop, calls=%fused_computation.1 | loop fusion | flops 524288 | bytes 3145728 | tf_op jit(solution)/shard_map/convert_element_type | solution.py:79
  172.0 11.4 %copy.58 = f32[16,16,16,128]{3,2,1,0:T(8,128)} copy(f32[16,16,16,128]{2,1,3,0:T(8,128)} %convert_bitcast_fusion) | data formatting | bytes 4194304 | tf_op jit(solution)/shard_map/convert_element_type | solution.py:79
  196.0 9.5 %fusion.29 = (f32[2048]{0:T(1024)S(1)}, f32[2048,256]{1,0:T(8,128)}) fusion(f32[256]{0:T(256)S(1)} %copy-done.13, bf16[256,1024]{1,0:T(8,128)(2,1)S(1)} %copy-done, f32[2048,1024]{1,0:T(8,128)} %copy-done.6, bf16[1024,256]{1,0:T(8,128)(2,1)S(1)} %copy-done.15, f32[2048,256]{1,0:T(8,128)} %fusion.71), kind=kOutput, calls=%fused_computation.48 | convolution fusion | flops 2188376064 | bytes 13640704 | tf_op jit(solution)/shard_map/dot_general | solution.py:115
  216.6 17.1 %all_to_all.49 = bf16[256,16,128]{2,1,0:T(8,128)(2,1)S(1)} all-to-all(bf16[256,16,128]{2,1,0:T(8,128)(2,1)S(1)} %get-tuple-element.2), channel_id=1, replica_groups=mesh['agent'=8,'chan'=8,'batch'=2] {'chan','batch'}, dimensions={0} | all-to-all | bytes 2097152 | tf_op jit(solution)/shard_map/all_to_all | solution.py:45
  234.3 7.0 %convolution_bitcast_fusion = f32[2048,256]{0,1:T(8,128)} fusion(bf16[2048,2048]{1,0:T(8,128)(2,1)} %param.13, bf16[32,8,16,128]{3,2,1,0:T(8,128)(2,1)S(1)} %bitcast.135), kind=kOutput, calls=%fused_computation.22 | convolution fusion | flops 2147483648 | bytes 11534336 | tf_op jit(solution)/shard_map/dot_general | solution.py:54
  241.4 70.7 %all-reduce.5.cloned.1.call-done = f32[2048,256]{0,1:T(8,128)} async-done(((f32[2048,256]{0,1:T(8,128)}), f32[2048,256]{0,1:T(8,128)}) %all-reduce.5.cloned.1.call-update) | async-done | bytes 2097168 | tf_op jit(solution)/shard_map/psum | solution.py:57
  312.1 7.8 %convolution_convert_fusion = bf16[256,2048]{1,0:T(8,128)(2,1)S(1)} fusion(bf16[2048,2048]{1,0:T(8,128)(2,1)} %param.12, f32[2048,256]{0,1:T(8,128)} %all-reduce.5.cloned.1.call-done, f32[2048,256]{0,1:T(8,128)} %all-reduce.3.cloned.1.call-done), kind=kOutput, calls=%fused_computation.26 | convolution fusion | flops 2157969408 | bytes 13631488 | tf_op jit(solution)/shard_map/dot_general | solution.py:61
  319.9 8.5 %copy.65 = bf16[16,16,2048]{1,0,2:T(8,128)(2,1)} copy(bf16[16,16,2048]{2,1,0:T(8,128)(2,1)S(1)} %bitcast.132) | data formatting | bytes 2097152 | tf_op jit(solution)/shard_map/reshape | solution.py:128
  328.4 11.2 %reshape.154 = bf16[16,2,16384]{2,1,0:T(2,128)(2,1)} reshape(bf16[2048,16,16]{2,1,0:T(8,128)(2,1)} %bitcast.125) | data formatting | bytes 2097152
  339.7 6.7 %all-to-all-start.3 = ((bf16[16,2,16384]{2,1,0:T(2,128)(2,1)}), bf16[16,2,16384]{2,1,0:T(2,128)(2,1)S(1)}, u32[]{:S(2)}, u32[]{:S(2)}) async-start(bf16[16,2,16384]{2,1,0:T(2,128)(2,1)} %reshape.154), calls=%async_computation.3 | async-start | bytes 2097152 | tf_op jit(solution)/shard_map/all_to_all | solution.py:49
  346.7 15.1 %psum.30 = f32[256,8]{0,1:T(8,128)S(1)} all-reduce(f32[256,8]{0,1:T(8,128)S(1)} %fusion.69), channel_id=1, replica_groups=mesh['agent'=8,'chan'=8,'batch'=2] {'agent'}, use_global_device_ids=true, to_apply=%region_12.13 | all-reduce | flops 2048 | bytes 16384 | tf_op jit(solution)/shard_map/psum | solution.py:105
  361.8 34.0 %psum.31 = f32[256,8]{0,1:T(8,128)S(1)} all-reduce(f32[256,8]{0,1:T(8,128)S(1)} %psum.30), channel_id=1, replica_groups=mesh['agent'=8,'chan'=8,'batch'=2] {'chan','batch'}, use_global_device_ids=true, to_apply=%region_13.14 | all-reduce | flops 2048 | bytes 16384 | tf_op jit(solution)/shard_map/psum | solution.py:105
  396.4 7.5 %reshape.155 = bf16[2048,16,16]{2,1,0:T(8,128)(2,1)} reshape(bf16[16,2,16384]{2,1,0:T(2,128)(2,1)S(1)} %all-to-all-done.3) | data formatting | bytes 2097152
  403.9 10.9 %convert_bitcast_fusion.1 = f32[16,16,16,128]{2,1,3,0:T(8,128)} fusion(bf16[2048,16,16]{2,1,0:T(8,128)(2,1)} %reshape.155), kind=kLoop, calls=%fused_computation.2 | loop fusion | flops 524288 | bytes 3145728 | tf_op jit(solution)/shard_map/convert_element_type | solution.py:132
  420.6 11.5 %copy.66 = f32[16,16,16,128]{3,2,1,0:T(8,128)} copy(f32[16,16,16,128]{2,1,3,0:T(8,128)} %convert_bitcast_fusion.1) | data formatting | bytes 4194304 | tf_op jit(solution)/shard_map/convert_element_type | solution.py:132
  (77 shorter events, 42.2 us)
Async XLA Ops:
  7.2 181.3 %copy-start = (bf16[256,1024]{1,0:T(8,128)(2,1)S(1)}, bf16[256,1024]{1,0:T(8,128)(2,1)}, u32[]{:S(2)}) copy-start(bf16[256,1024]{1,0:T(8,128)(2,1)} %param.15) | copy-start | bytes 1572868
  7.2 3.2 copy-start.2
  7.2 3.2 copy-start.12
  7.2 98.9 %all-reduce.3.cloned.1.call-start = ((), (), s32[]{:S(2)}) async-start(), calls=%async_computation.4 | async-start | bytes 4194304 | tf_op jit(solution)/shard_map/psum | solution.py:57
  132.4 6.9 %copy-start.14 = (s32[16,128]{1,0:T(8,128)S(1)}, s32[16,128]{1,0:T(8,128)}, u32[]{:S(2)}) copy-start(s32[16,128]{1,0:T(8,128)} %param.18) | copy-start | bytes 24580
  132.4 7.0 %copy-start.16 = (s32[128]{0:T(128)S(1)}, s32[128]{0:T(128)}, u32[]{:S(2)}) copy-start(s32[128]{0:T(128)} %param.19) | copy-start | bytes 1540
  132.4 21.2 %all-to-all-start.1 = ((bf16[16,2,16384]{2,1,0:T(2,128)(2,1)}), bf16[16,2,16384]{2,1,0:T(2,128)(2,1)S(1)}, u32[]{:S(2)}, u32[]{:S(2)}) async-start(bf16[16,2,16384]{2,1,0:T(2,128)(2,1)} %reshape.152), calls=%async_computation.1 | async-start | bytes 2097152 | tf_op jit(solution)/shard_map/all_to_all | solution.py:49
  139.0 173.0 %all-reduce.5.cloned.1.call-start = ((), (), s32[]{:S(2)}) async-start(), calls=%async_computation.5 | async-start | bytes 4194304 | tf_op jit(solution)/shard_map/psum | solution.py:57
  187.4 0.7 copy-start.13
  188.5 1.6 copy-start.10
  188.5 1.7 copy-start.15
  189.8 3.3 copy-start.6
  190.1 3.0 copy-start.11
  193.2 1.0 copy-start.8
  211.7 2.2 copy-start.4
  211.7 2.9 copy-start.7
  339.7 6.8 %copy-start.9 = (bf16[256,2048]{0,1:T(8,128)(2,1)S(1)}, bf16[256,2048]{0,1:T(8,128)(2,1)}, u32[]{:S(2)}) copy-start(bf16[256,2048]{0,1:T(8,128)(2,1)} %copy-done.8) | copy-start | bytes 3145732
  339.7 56.7 %all-to-all-start.3 = ((bf16[16,2,16384]{2,1,0:T(2,128)(2,1)}), bf16[16,2,16384]{2,1,0:T(2,128)(2,1)S(1)}, u32[]{:S(2)}, u32[]{:S(2)}) async-start(bf16[16,2,16384]{2,1,0:T(2,128)(2,1)} %reshape.154), calls=%async_computation.3 | async-start | bytes 2097152 | tf_op jit(solution)/shard_map/all_to_all | solution.py:49
  420.6 11.5 %copy-start.3 = (bf16[256,16,128]{2,1,0:T(8,128)(2,1)S(1)}, bf16[256,16,128]{2,1,0:T(8,128)(2,1)}, u32[]{:S(2)}) copy-start(bf16[256,16,128]{2,1,0:T(8,128)(2,1)} %param.10) | copy-start | bytes 3145732
  432.1 2.2 copy-start.5
  434.3 3.6 copy-start.1
Sparse Core Ops, SparseCore 0:
  42.2 63.8 all-reduce.2
  241.5 70.5 all-reduce.4
